TPU v7x, 256 devices: a whole 4x4x8 slice. The times are simulated.
256 devices in a mesh: strip: 64 (over x, z, core), chan: 4 (over y).
Axes of the slice: x: 4, y: 4, z: 8, core: 2. Of those that a mesh axis runs over, the one named last changes fastest.
Arguments:
- section_input: bfloat16 [48, 8192, 256], P(None, 'strip'), may hold values from -6 to 6
- conv_weight: bfloat16 [3, 3, 256, 256], replicated, may hold values from -0.125 to 0.125
- conv_bias: float32 [256], replicated, may hold values from -3 to 3
- deep_weight: bfloat16 [3, 3, 256, 512], P(None, None, None, 'chan'), may hold values from -0.125 to 0.125
- deep_bias: float32 [512], P('chan'), may hold values from -3 to 3
- labels: int32 [24, 4096], P(None, 'strip'), may hold values from 0 to 32, as said below
- slot_ids: int32 [2048], P('strip'), may hold values from 0 to 4095, as said below
- embed_grad: float32 [4096, 512], P('strip', 'chan'), may hold values from -0.8 to 0.8
Outputs:
- embeddings: float32 [4096, 512], P('strip', 'chan')
- weight_grad: float32 [3, 3, 256, 512], P(None, None, None, 'chan')
- bias_grad: float32 [512], P('chan')
Inputs may be any that keep to these rules, and one draw needn't show every extreme that they name: `labels`: the value 32 marks background; any other value v names entry v of the list of the strip that holds the pixel. `slot_ids`: A value s names slot s % 64 of owner s // 64 (an index of strip). The slots within one strip's list differ; a slot stands in the lists of at most two strips, which are neighbours (a crack across a strip border). Every owner holds at most 64 components and some owner holds exactly 64.
All inputs are finite; a program needn't handle non-finite values.
Results may differ from a plain program's by a relative error of at most 0.0035.
Values may be sent and summed in bfloat16 or wider, within the bound.
A program may use at most 64 MiB of HBM per device.

v0:
```python
import jax
import jax.numpy as jnp
from jax import lax
from jax.sharding import PartitionSpec as P


def with_halo(cells, sides, width):
    for axis, dim in sides:
        count = lax.axis_size(axis)
        ends = count - 1
        head = lax.slice_in_dim(cells, 0, width, axis=dim)
        tail = lax.slice_in_dim(cells, cells.shape[dim] - width, cells.shape[dim], axis=dim)
        cells = jnp.concatenate(
            [
                lax.ppermute(tail, axis, [(i, (i + 1) % count) for i in range(ends)]),
                cells,
                lax.ppermute(head, axis, [((i + 1) % count, i) for i in range(ends)]),
            ],
            axis=dim,
        )
    return cells


def swish(value):
    return value * jax.nn.sigmoid(value)


def swish_slope(value):
    sigma = jax.nn.sigmoid(value)
    return sigma * (1.0 + value * (1.0 - sigma))


def convolve(padded, weight, row_count, col_count):
    channels = padded.shape[-1]
    running = None
    for shift_row in range(3):
        for shift_col in range(3):
            window = padded[
                shift_row : shift_row + row_count, shift_col : shift_col + col_count
            ].reshape(row_count * col_count, channels)
            partial_term = jnp.dot(
                window, weight[shift_row, shift_col], preferred_element_type=jnp.float32
            )
            running = partial_term if running is None else running + partial_term
    return running.reshape(row_count, col_count, weight.shape[-1])


def pool_pairs(hidden):
    row_count, col_count, channels = hidden.shape
    return (
        hidden.reshape(row_count // 2, 2, col_count // 2, 2, channels)
        .mean(axis=(1, 3))
        .astype(jnp.bfloat16)
    )


def body(
    section_input, conv_weight, conv_bias, deep_weight, deep_bias, labels, slot_ids, embed_grad
):
    chan_count = lax.axis_size("chan")
    chan_pos = lax.axis_index("chan")
    strip_count = lax.axis_size("strip")
    strip_pos = lax.axis_index("strip")
    row_total, col_local, channels = section_input.shape
    row_part = row_total // chan_count
    half_cols = col_local // 2
    padded_rows = jnp.pad(section_input, ((1, 1), (0, 0), (0, 0)))
    own_rows = lax.dynamic_slice_in_dim(padded_rows, chan_pos * row_part, row_part + 2, 0)
    extended = with_halo(own_rows, (("strip", 1),), 3)
    hidden = swish(convolve(extended, conv_weight, row_part, col_local + 4) + conv_bias)
    pooled = pool_pairs(hidden)
    column = jnp.arange(half_cols + 2)
    outside = (column == 0) & (strip_pos == 0) | (column == half_cols + 1) & (
        strip_pos == strip_count - 1
    )
    pooled = jnp.where(outside[None, :, None], jnp.zeros_like(pooled), pooled)
    gathered = lax.all_gather(pooled, "chan", axis=0, tiled=True)
    padded_deep = jnp.pad(gathered, ((1, 1), (0, 0), (0, 0)))
    half_rows = gathered.shape[0]
    deep_pre = convolve(padded_deep, deep_weight, half_rows, half_cols) + deep_bias
    width_deep = deep_weight.shape[-1]
    features = swish(deep_pre).astype(jnp.bfloat16).reshape(-1, width_deep)
    flat_labels = labels.reshape(-1)
    list_len = slot_ids.shape[0]
    member = flat_labels[None, :] == jnp.arange(list_len, dtype=jnp.int32)[:, None]
    part_sums = jnp.dot(member.astype(jnp.bfloat16), features, preferred_element_type=jnp.float32)
    part_counts = jnp.sum(member.astype(jnp.float32), axis=1)
    owned = embed_grad.shape[0]
    dense_sums = (
        jnp.zeros((owned * strip_count, width_deep), jnp.float32).at[slot_ids].set(part_sums)
    )
    dense_counts = jnp.zeros((owned * strip_count,), jnp.float32).at[slot_ids].set(part_counts)
    slot_sums, slot_counts = (
        lax.psum_scatter(dense_sums, "strip", scatter_dimension=0, tiled=True),
        lax.psum_scatter(dense_counts, "strip", scatter_dimension=0, tiled=True),
    )
    divisor = jnp.maximum(slot_counts, 1.0)[:, None]
    embeddings = slot_sums / divisor
    every_grad = lax.all_gather(embed_grad / divisor, "strip", axis=0, tiled=True)
    entry_grad = every_grad[slot_ids]
    pixel_grad = lax.dot_general(
        member.astype(jnp.float32),
        entry_grad,
        (((0,), (0,)), ((), ())),
        precision=lax.Precision.HIGHEST,
        preferred_element_type=jnp.float32,
    )
    deep_grad = (pixel_grad * swish_slope(deep_pre.reshape(-1, width_deep))).astype(jnp.bfloat16)
    pieces = []
    for shift_row in range(3):
        for shift_col in range(3):
            window = padded_deep[
                shift_row : shift_row + half_rows, shift_col : shift_col + half_cols
            ].reshape(-1, channels)
            pieces.append(
                lax.dot_general(
                    window, deep_grad, (((0,), (0,)), ((), ())), preferred_element_type=jnp.float32
                )
            )
    local_weight = jnp.stack(pieces).reshape(3, 3, channels, width_deep)
    local_bias = jnp.sum(deep_grad.astype(jnp.float32), axis=0)
    weight_grad, bias_grad = lax.psum((local_weight, local_bias), "strip")
    return (embeddings, weight_grad, bias_grad)


def solution(mesh):
    placed = (
        P(None, "strip", None),
        P(),
        P(),
        P(None, None, None, "chan"),
        P("chan"),
        P(None, "strip"),
        P("strip"),
        P("strip", "chan"),
    )
    return jax.shard_map(
        body,
        mesh=mesh,
        in_specs=placed,
        out_specs=(P("strip", "chan"), P(None, None, None, "chan"), P("chan")),
        check_vma=False,
    )
```

profile of v0, /device:TPU:8, one launch (start us, length us, event | category | flops | bytes accessed | tf_op | source)
XLA Modules:
  0.0 597.8 jit_solution(9862695185246819074)
XLA Ops:
  8.3 1.3 collective-permute-start.1
  9.6 3.0 collective-permute-start
  13.8 1.6 pad_maximum_fusion
  15.4 2.6 fusion.59
  17.9 2.1 reshape.94
  20.0 2.0 reshape.93
  22.0 2.1 reshape.95
  24.1 2.1 reshape.96
  26.1 2.1 reshape.97
  29.2 1.0 reshape.99
  30.4 1.1 reshape.101
  31.5 1.4 fusion.23
  41.7 2.7 fusion.2
  44.5 15.0 %all_gather.6 = bf16[24,66,256]{2,1,0:T(8,128)(2,1)S(1)} all-gather(bf16[6,66,256]{2,1,0:T(8,128)(2,1)S(1)} %fusion.15), channel_id=1, replica_groups=mesh['strip'=64,'chan'=4] {'chan'}, dimensions={0}, use_global_device_ids=true | all-gather | bytes 1013760 | tf_op jit(solution)/shard_map/all_gather | solution.py:77
  59.5 1.4 pad_slice_fusion
  66.5 2.1 scatter_custom_fusion
  70.7 251.7 %all-reduce.2 = f32[4096]{0:T(1024)S(1)} all-reduce(f32[4096]{0:T(1024)S(1)} %scatter_custom_fusion.1), channel_id=3, replica_groups=mesh['strip'=64,'chan'=4] {'strip'}, use_global_device_ids=true, to_apply=%region_5.6.clone | all-reduce | flops 4096 | bytes 32768
  322.5 1.5 broadcast_divide_fusion
  324.1 70.7 %all-gather.2.cloned.1.call-done = f32[4096,128]{1,0:T(8,128)} async-done(((f32[64,128]{1,0:T(8,128)}), f32[4096,128]{1,0:T(8,128)}) %all-gather.2.cloned.1.call-update) | async-done | bytes 2097168 | tf_op jit(solution)/shard_map/all_gather | solution.py:99
  394.8 2.2 gather_fusion
  397.0 2.1 convert_reduce_fusion
  404.5 127.1 %psum.15 = f32[128]{0:T(128)} all-reduce(f32[128]{0:T(128)S(1)} %get-tuple-element.25), channel_id=1, replica_groups=mesh['strip'=64,'chan'=4] {'strip'}, use_global_device_ids=true, to_apply=%region_8.9 | all-reduce | flops 128 | bytes 1024 | tf_op jit(solution)/shard_map/psum | solution.py:122
  531.6 57.3 %all-reduce.5.cloned.1.call-done = f32[3,3,256,128]{3,2,1,0:T(8,128)} async-done(((f32[3,3,256,128]{3,2,1,0:T(8,128)}), f32[3,3,256,128]{3,2,1,0:T(8,128)}) %all-reduce.5.cloned.1.call-update) | async-done | bytes 1179664 | tf_op jit(solution)/shard_map/psum | solution.py:122
  588.9 2.4 copy.20
  (108 shorter events, 24.5 us)
Async XLA Ops:
  7.2 5.5 copy-start
  7.2 315.3 %reduce-scatter.2.cloned.1.call-start = ((), (), s32[]{:S(2)}) async-start(), calls=%async_computation.1 | async-start | bytes 2129920 | tf_op jit(solution)/shard_map/reduce_scatter | solution.py:94
  8.3 5.5 collective-permute-start.1
  9.6 4.1 copy-start.27
  9.6 4.1 copy-start.24
  9.6 4.2 collective-permute-start
  30.3 1.2 copy-start.11
  31.5 1.4 copy-start.18
  31.5 1.6 copy-start.20
  33.1 1.1 copy-start.17
  34.2 1.1 copy-start.16
  39.2 1.1 copy-start.12
  59.5 1.5 copy-start.22
  60.9 1.4 copy-start.5
  60.9 1.7 copy-start.3
  61.0 2.1 copy-start.1
  66.4 3.0 copy-start.28
  66.4 256.1 %copy-start.23 = (f32[64,128]{1,0:T(8,128)S(1)}, f32[64,128]{1,0:T(8,128)}, u32[]{:S(2)}) copy-start(f32[64,128]{1,0:T(8,128)} %param.15) | copy-start | bytes 98308
  68.6 326.2 %all-gather.2.cloned.1.call-start = ((), (), s32[]{:S(2)}) async-start(), calls=%async_computation.2 | async-start | bytes 2129920 | tf_op jit(solution)/shard_map/all_gather | solution.py:99
  324.0 264.9 %all-reduce.5.cloned.1.call-start = ((), (), s32[]{:S(2)}) async-start(), calls=%async_computation.3 | async-start | bytes 2359296 | tf_op jit(solution)/shard_map/psum | solution.py:122
  396.9 2.1 copy-start.10
  397.0 2.5 copy-start.8
  399.5 1.2 copy-start.4
  400.2 1.2 copy-start.2
  (10 other events, 10.1 us)
Sparse Core Ops, SparseCore 0:
  68.7 145.5 reduce-scatter.1
  324.1 70.6 all-gather.1
  404.6 184.2 all-reduce.4
where the time goes:
time: 599 us; the launch traced here: 598 us
  blocking collectives  394 us (66%)
  waiting for transfers between devices  128 us (21%)
  local copies, waits for them, and re-layouts  36.6 us (6%)
  between operations  14.9 us (2%)
  matrix products  13.8 us (2%)
  other arithmetic  6.09 us (1%)
    unnamed x1, blocking collectives  252 us
    psum x1, blocking collectives, body(): weight_grad, bias_grad = lax.psum((local_weight, local_bias), 'strip')  127 us
    all_gather x1, waiting for transfers between devices, body(): lax.all_gather(embed_grad / divisor, 'strip', axis=0, tiled=True)  70.7 us
    psum x1, waiting for transfers between devices, body(): weight_grad, bias_grad = lax.psum((local_weight, local_bias), 'strip')  57.3 us
    all_gather x1, blocking collectives, body(): gathered = lax.all_gather(pooled, 'chan', axis=0, tiled=True)  15 us
    reshape x9, local copies, waits for them, and re-layouts, convolve(): window = padded[shift_row:shift_row + row_count, shift_col:shift_col + co...  13.6 us
  transfers between devices with their start and end apart: 5, of which 2 were waited for; matrix products, arithmetic and copies ran while one was open for 0% of the time, Pallas kernels for 0%

commit v1 on v0

--- a/solution.py
+++ b/solution.py
@@ -96,7 +96,10 @@
     )
     divisor = jnp.maximum(slot_counts, 1.0)[:, None]
     embeddings = slot_sums / divisor
-    every_grad = lax.all_gather(embed_grad / divisor, "strip", axis=0, tiled=True)
+    every_grad = jnp.concatenate(
+        lax.all_to_all(jnp.stack([embed_grad / divisor] * lax.axis_size("strip")), "strip", 0, 0),
+        axis=0,
+    )
     entry_grad = every_grad[slot_ids]
     pixel_grad = lax.dot_general(
         member.astype(jnp.float32),

time: 599 us -> 585 us (0.977)
  waiting for transfers between devices: 128 us -> 109 us
    all_gather x1 -> x0, waiting for transfers between devices: 70.7 us -> none  [body(): lax.all_gather(embed_grad / divisor, 'strip', axis=0, tiled=True)]
    all_to_all x0 -> x1, waiting for transfers between devices: none -> 51 us  [body(): lax.all_to_all(jnp.stack([embed_grad / divisor] * lax.axis_size('strip'))...]
where the time goes in v1:
time: 585 us; the launch traced here: 584 us
  blocking collectives  392 us (67%)
  waiting for transfers between devices  109 us (19%)
  local copies, waits for them, and re-layouts  38.3 us (7%)
  between operations  15.2 us (3%)
  matrix products  13.8 us (2%)
  starting transfers between devices  9.97 us (2%)
  other arithmetic  6.08 us (1%)
    unnamed x1, blocking collectives  252 us
    psum x1, blocking collectives, body(): weight_grad, bias_grad = lax.psum((local_weight, local_bias), 'strip')  125 us
    psum x1, waiting for transfers between devices, body(): weight_grad, bias_grad = lax.psum((local_weight, local_bias), 'strip')  57.6 us
    all_to_all x1, waiting for transfers between devices, body(): lax.all_to_all(jnp.stack([embed_grad / divisor] * lax.axis_size('strip'))...  51 us
    all_gather x1, blocking collectives, body(): gathered = lax.all_gather(pooled, 'chan', axis=0, tiled=True)  15.1 us
    reshape x9, local copies, waits for them, and re-layouts, convolve(): window = padded[shift_row:shift_row + row_count, shift_col:shift_col + co...  13.6 us
  transfers between devices with their start and end apart: 5, of which 2 were waited for; matrix products, arithmetic and copies ran while one was open for 0% of the time, Pallas kernels for 0%

profile of v1, /device:TPU:8, one launch (start us, length us, event | category | flops | bytes accessed | tf_op | source)
XLA Modules:
  0.0 583.9 jit_solution(12276055326656072925)
XLA Ops:
  8.3 1.3 collective-permute-start.1
  9.6 3.0 collective-permute-start
  13.8 1.6 pad_maximum_fusion
  15.4 2.5 fusion.59
  17.9 2.1 reshape.99
  20.0 2.0 reshape.98
  22.0 2.1 reshape.100
  24.1 2.1 reshape.101
  26.2 2.0 reshape.102
  31.5 1.4 fusion.23
  41.7 2.7 fusion.2
  44.5 15.1 %all_gather.3 = bf16[24,66,256]{2,1,0:T(8,128)(2,1)S(1)} all-gather(bf16[6,66,256]{2,1,0:T(8,128)(2,1)S(1)} %fusion.15), channel_id=1, replica_groups=mesh['strip'=64,'chan'=4] {'chan'}, dimensions={0}, use_global_device_ids=true | all-gather | bytes 1013760 | tf_op jit(solution)/shard_map/all_gather | solution.py:77
  59.6 1.4 pad_slice_fusion
  66.6 2.1 scatter_custom_fusion
  70.8 251.7 %all-reduce.2 = f32[4096]{0:T(1024)S(1)} all-reduce(f32[4096]{0:T(1024)S(1)} %scatter_custom_fusion.1), channel_id=3, replica_groups=mesh['strip'=64,'chan'=4] {'strip'}, use_global_device_ids=true, to_apply=%region_5.6.clone | all-reduce | flops 4096 | bytes 32768
  322.6 1.5 broadcast_divide_fusion
  324.0 1.6 stack.22
  325.6 5.6 all-to-all-start
  331.2 51.0 %all-to-all-done = f32[64,64,128]{2,1,0:T(8,128)} async-done(((f32[64,64,128]{2,1,0:T(8,128)}), f32[64,64,128]{2,1,0:T(8,128)}, u32[]{:S(2)}, u32[]{:S(2)}) %all-to-all-start) | async-done | bytes 2097184 | tf_op jit(solution)/shard_map/all_to_all | solution.py:100
  382.2 2.2 gather_fusion
  384.4 2.1 convert_reduce_fusion
  391.9 125.2 %psum.15 = f32[128]{0:T(128)} all-reduce(f32[128]{0:T(128)S(1)} %get-tuple-element.25), channel_id=1, replica_groups=mesh['strip'=64,'chan'=4] {'strip'}, use_global_device_ids=true, to_apply=%region_8.9 | all-reduce | flops 128 | bytes 1024 | tf_op jit(solution)/shard_map/psum | solution.py:125
  517.1 57.6 %all-reduce.5.cloned.1.call-done = f32[3,3,256,128]{3,2,1,0:T(8,128)} async-done(((f32[3,3,256,128]{3,2,1,0:T(8,128)}), f32[3,3,256,128]{3,2,1,0:T(8,128)}) %all-reduce.5.cloned.1.call-update) | async-done | bytes 1179664 | tf_op jit(solution)/shard_map/psum | solution.py:125
  574.7 2.4 copy.20
  (108 shorter events, 26.6 us)
Async XLA Ops:
  7.2 5.5 copy-start
  7.2 315.4 %reduce-scatter.2.cloned.1.call-start = ((), (), s32[]{:S(2)}) async-start(), calls=%async_computation.2 | async-start | bytes 2129920 | tf_op jit(solution)/shard_map/reduce_scatter | solution.py:94
  8.3 5.5 collective-permute-start.1
  9.6 4.1 copy-start.27
  9.6 4.1 copy-start.24
  9.6 4.2 collective-permute-start
  30.3 1.2 copy-start.11
  31.5 1.4 copy-start.18
  31.5 1.6 copy-start.20
  33.1 1.1 copy-start.17
  34.2 1.1 copy-start.16
  39.2 1.1 copy-start.12
  59.6 1.5 copy-start.22
  61.0 1.4 copy-start.5
  61.0 1.8 copy-start.3
  61.0 2.2 copy-start.1
  66.5 3.0 copy-start.28
  66.6 256.0 %copy-start.23 = (f32[64,128]{1,0:T(8,128)S(1)}, f32[64,128]{1,0:T(8,128)}, u32[]{:S(2)}) copy-start(f32[64,128]{1,0:T(8,128)} %param.15) | copy-start | bytes 98308
  325.6 56.6 %all-to-all-start = ((f32[64,64,128]{2,1,0:T(8,128)}), f32[64,64,128]{2,1,0:T(8,128)}, u32[]{:S(2)}, u32[]{:S(2)}) async-start(f32[64,64,128]{2,1,0:T(8,128)} %stack.22), calls=%async_computation.1 | async-start | bytes 4194304 | tf_op jit(solution)/shard_map/all_to_all | solution.py:100
  331.2 243.6 %all-reduce.5.cloned.1.call-start = ((), (), s32[]{:S(2)}) async-start(), calls=%async_computation.3 | async-start | bytes 2359296 | tf_op jit(solution)/shard_map/psum | solution.py:125
  384.4 2.1 copy-start.10
  384.4 2.5 copy-start.8
  386.9 1.2 copy-start.4
  387.6 1.2 copy-start.2
  (10 other events, 10.2 us)
Sparse Core Ops, SparseCore 0:
  68.8 145.4 reduce-scatter.1
  392.0 182.6 all-reduce.4
